TPU v7x, 512 devices: a whole 4x4x16 slice. The times are simulated.
512 devices in a mesh: gx: 32 (over x, z_lo, core), gy: 16 (over z_hi, y).
Axes of the slice: x: 4, y: 4, z: 16 (z_hi: 4, z_lo: 4; z = z_hi * 4 + z_lo), core: 2. Of those that a mesh axis runs over, the one named last changes fastest.
Arguments:
- points: bfloat16 [524288, 64], P(('gx', 'gy')), may hold values from -6 to 6
- pivots: int32 [2, 128], replicated, may hold values from 0 to 1023, as said below
- owners: int32 [2], replicated, may hold values from 0 to 511
- coeffs: float32 [256, 64], replicated, may hold values from -6 to 6
- noise: float32 [524288, 64], P(('gx', 'gy')), may hold values from -4 to 4
Outputs:
- kernel_probes: float32 [524288, 64], P(('gx', 'gy'))
- factor: float32 [524288, 256], P(('gx', 'gy'))
Inputs may be any that keep to these rules, and one draw needn't show every extreme that they name: `pivots`: the two rows together hold 256 distinct indices, among them 0 and 1023.
All inputs are finite; a program needn't handle non-finite values.
Results may differ from a plain program's by a relative error of at most 0.0003.
Values may be sent and summed in bfloat16 or wider, within the bound.
A program may use at most 64 MiB of HBM per device.

v0:
```python
import jax
import jax.numpy as jnp
from jax import lax
from jax.sharding import PartitionSpec as P

PIVOTS = 128
KERNEL_SCALE = 32


jitter = 0.1
noise_weight = 0.5


def spread(value, axis, source):
    kept = jnp.where(lax.axis_index(axis) == source, value, 0).astype(value.dtype)
    return lax.psum(kept, axis)


def passed_along(value, axis, steps):
    count = lax.axis_size(axis)
    pairs = [(source, (source + steps) % count) for source in range(count)]
    return lax.ppermute(value, axis, pairs)


def kern(left, right):
    left_square_norm = jnp.sum(jnp.square(left.astype(jnp.float32)), axis=1)
    right_square_norm = jnp.sum(jnp.square(right.astype(jnp.float32)), axis=1)
    cross_term = jnp.dot(left, right.T, preferred_element_type=jnp.float32)
    return jnp.exp(
        -(left_square_norm[:, None] + right_square_norm[None, :] - 2.0 * cross_term)
        / (1.0 * KERNEL_SCALE)
    )


def shards(points, pivots, owners, coeffs, noise):
    hp = lax.Precision.HIGHEST
    solve = jax.scipy.linalg.solve_triangular
    width = points.shape[1]
    count = points.shape[0]
    ident = jnp.eye(PIVOTS, dtype=jnp.float32)
    first = spread(points[pivots[0]], ("gx", "gy"), owners[0])
    second = spread(points[pivots[1]], ("gx", "gy"), owners[1])
    chol_one = jnp.linalg.cholesky(kern(first, first) + jitter * ident)
    first_cols = solve(chol_one, kern(points, first).T, lower=True).T
    rows = spread(first_cols[pivots[1]], ("gx", "gy"), owners[1])
    chol_two = jnp.linalg.cholesky(
        kern(second, second) - jnp.dot(rows, rows.T, precision=hp) + jitter * ident
    )
    residual_cols = kern(points, second) - jnp.dot(first_cols, rows.T, precision=hp)
    second_cols = solve(chol_two, residual_cols.T, lower=True).T
    factor = jnp.concatenate([first_cols, second_cols], axis=1)
    probes = jnp.dot(factor, coeffs, precision=hp, preferred_element_type=jnp.float32) + noise
    packed = jnp.concatenate([points, probes.astype(jnp.bfloat16)], axis=1)

    def contribute(total, piece):
        tile = kern(points, piece[:, :width]).astype(jnp.bfloat16)
        return total + jnp.dot(tile, piece[:, width:], preferred_element_type=jnp.float32)

    total = contribute(jnp.zeros((count, probes.shape[1]), jnp.float32), packed)
    piece = passed_along(packed, ("gx", "gy"), -3)
    total = contribute(total, piece)
    for stop_index in range(5):
        if stop_index == 2:
            piece = passed_along(piece, ("gx", "gy"), 2)
        else:
            piece = passed_along(piece, ("gx", "gy"), 1)
        total = contribute(total, piece)
    kernel_probes = total / jnp.sqrt(1.0 * count) + noise_weight * probes
    return (kernel_probes, factor)


def solution(mesh):
    in_specs = (P(("gx", "gy"), None), P(), P(), P(), P(("gx", "gy"), None))
    out_specs = (P(("gx", "gy"), None), P(("gx", "gy"), None))
    return jax.shard_map(shards, mesh=mesh, in_specs=in_specs, out_specs=out_specs, check_vma=False)
```

profile of v0, /device:TPU:225, one launch (start us, length us, event | category | flops | bytes accessed | tf_op | source)
XLA Modules:
  0.0 789.9 jit_solution(290399929009579966)
XLA Ops:
  14.1 104.2 %all-reduce = (bf16[128,64]{1,0:T(8,128)(2,1)S(1)}, bf16[128,64]{1,0:T(8,128)(2,1)S(1)}) all-reduce(bf16[128,64]{1,0:T(8,128)(2,1)S(1)} %broadcast_select_fusion.1, bf16[128,64]{1,0:T(8,128)(2,1)S(1)} %broadcast_select_fusion.2), channel_id=1, replica_groups=mesh['gx'=32,'gy'=16] {'gx','gy'}, use_global_device_ids=true, to_apply=%region_5.0 | all-reduce | flops 16384 | bytes 65536 | tf_op jit(solution)/shard_map/psum | solution.py:16
  119.0 11.7 %cholesky.44 = f32[128,128]{1,0:T(8,128)S(1)} custom-call(f32[128,128]{1,0:T(8,128)S(1)} %fusion.81), custom_call_target="Cholesky" | custom-call | tf_op jit(solution)/shard_map/jit(cholesky)/cholesky | solution.py:43
  132.0 9.8 %custom-call.6 = f32[1,128,128]{1,2,0:T(8,128)S(1)} custom-call(f32[1,128,128]{2,1,0:T(8,128)S(1)} %fusion.75), custom_call_target="InvertDiagBlocksLowerTriangular" | custom-call | tf_op jit(solution)/shard_map/jit(_solve_triangular)/triangular_solve | solution.py:44
  144.6 436.6 %all-reduce.3.cloned.1.call-done = f32[128,128]{0,1:T(8,128)} async-done(((f32[128,128]{0,1:T(8,128)}), f32[128,128]{0,1:T(8,128)}) %all-reduce.3.cloned.1.call-update) | async-done | bytes 65552 | tf_op jit(solution)/shard_map/psum | solution.py:16
  582.6 11.7 %cholesky.55 = f32[128,128]{1,0:T(8,128)S(1)} custom-call(f32[128,128]{1,0:T(8,128)S(1)} %fusion.78), custom_call_target="Cholesky" | custom-call | tf_op jit(solution)/shard_map/jit(cholesky)/cholesky | solution.py:46
  595.6 9.9 %custom-call.7 = f32[1,128,128]{1,2,0:T(8,128)S(1)} custom-call(f32[1,128,128]{2,1,0:T(8,128)S(1)} %fusion.76), custom_call_target="InvertDiagBlocksLowerTriangular" | custom-call | tf_op jit(solution)/shard_map/jit(_solve_triangular)/triangular_solve | solution.py:50
  609.4 9.5 %collective-permute-start = (bf16[1024,128]{0,1:T(8,128)(2,1)S(1)}, bf16[1024,128]{0,1:T(8,128)(2,1)S(1)}, u32[]{:S(2)}, u32[]{:S(2)}) collective-permute-start(bf16[1024,128]{0,1:T(8,128)(2,1)S(1)} %pad_maximum_fusion.1), channel_id=1, source_target_pairs={{0,509},{1,510},{2,511},{3,0},{4,1},{5,2},{6,3},{7,4},{8,5},{9,6},... | collective-permute-start | bytes 786440 | tf_op jit(solution)/shard_map/ppermute | solution.py:22
  621.7 9.1 %collective-permute-done = bf16[1024,128]{0,1:T(8,128)(2,1)S(1)} collective-permute-done((bf16[1024,128]{0,1:T(8,128)(2,1)S(1)}, bf16[1024,128]{0,1:T(8,128)(2,1)S(1)}, u32[]{:S(2)}, u32[]{:S(2)}) %collective-permute-start) | collective-permute-done | bytes 262176 | tf_op jit(solution)/shard_map/ppermute | solution.py:22
  630.9 12.1 %collective-permute-start.1 = (bf16[1024,128]{0,1:T(8,128)(2,1)S(1)}, bf16[1024,128]{0,1:T(8,128)(2,1)S(1)}, u32[]{:S(2)}, u32[]{:S(2)}) collective-permute-start(bf16[1024,128]{0,1:T(8,128)(2,1)S(1)} %collective-permute-done), channel_id=1, source_target_pairs={{0,1},{1,2},{2,3},{3,4},{4,5},{5,6},{6,7},{7,8},{8,9},{9,10},{10,1... | collective-permute-start | bytes 786440 | tf_op jit(solution)/shard_map/ppermute | solution.py:22
  643.0 1.6 fusion.46
  644.6 28.1 %collective-permute-done.1 = bf16[1024,128]{0,1:T(8,128)(2,1)S(1)} collective-permute-done((bf16[1024,128]{0,1:T(8,128)(2,1)S(1)}, bf16[1024,128]{0,1:T(8,128)(2,1)S(1)}, u32[]{:S(2)}, u32[]{:S(2)}) %collective-permute-start.1) | collective-permute-done | bytes 262176 | tf_op jit(solution)/shard_map/ppermute | solution.py:22
  672.7 1.9 collective-permute-start.2
  674.7 1.6 fusion.45
  676.3 34.9 %collective-permute-done.2 = bf16[1024,128]{0,1:T(8,128)(2,1)S(1)} collective-permute-done((bf16[1024,128]{0,1:T(8,128)(2,1)S(1)}, bf16[1024,128]{0,1:T(8,128)(2,1)S(1)}, u32[]{:S(2)}, u32[]{:S(2)}) %collective-permute-start.2) | collective-permute-done | bytes 262176 | tf_op jit(solution)/shard_map/ppermute | solution.py:22
  711.2 1.9 collective-permute-start.3
  713.1 1.6 fusion.44
  714.8 17.3 %collective-permute-done.3 = bf16[1024,128]{0,1:T(8,128)(2,1)S(1)} collective-permute-done((bf16[1024,128]{0,1:T(8,128)(2,1)S(1)}, bf16[1024,128]{0,1:T(8,128)(2,1)S(1)}, u32[]{:S(2)}, u32[]{:S(2)}) %collective-permute-start.3) | collective-permute-done | bytes 262176 | tf_op jit(solution)/shard_map/ppermute | solution.py:22
  732.1 1.9 collective-permute-start.4
  734.0 1.6 fusion.43
  735.6 23.9 %collective-permute-done.4 = bf16[1024,128]{0,1:T(8,128)(2,1)S(1)} collective-permute-done((bf16[1024,128]{0,1:T(8,128)(2,1)S(1)}, bf16[1024,128]{0,1:T(8,128)(2,1)S(1)}, u32[]{:S(2)}, u32[]{:S(2)}) %collective-permute-start.4) | collective-permute-done | bytes 262176 | tf_op jit(solution)/shard_map/ppermute | solution.py:22
  759.6 2.1 collective-permute-start.5
  761.7 1.6 fusion.42
  763.4 17.3 %collective-permute-done.5 = bf16[1024,128]{0,1:T(8,128)(2,1)S(1)} collective-permute-done((bf16[1024,128]{0,1:T(8,128)(2,1)S(1)}, bf16[1024,128]{0,1:T(8,128)(2,1)S(1)}, u32[]{:S(2)}, u32[]{:S(2)}) %collective-permute-start.5) | collective-permute-done | bytes 262176 | tf_op jit(solution)/shard_map/ppermute | solution.py:22
  780.7 2.4 fusion.41
  (52 shorter events, 19.8 us)
Async XLA Ops:
  7.2 600.6 %copy-start = (f32[256,64]{0,1:T(8,128)S(1)}, f32[256,64]{0,1:T(8,128)}, u32[]{:S(2)}) copy-start(f32[256,64]{0,1:T(8,128)} %param.11) | copy-start | bytes 196612
  7.2 111.4 %copy-start.1 = (bf16[1024,64]{0,1:T(8,128)(2,1)S(1)}, bf16[1024,64]{0,1:T(8,128)(2,1)}, u32[]{:S(2)}) copy-start(bf16[1024,64]{0,1:T(8,128)(2,1)} %param.8) | copy-start | bytes 393220
  7.2 574.1 %all-reduce.3.cloned.1.call-start = ((), (), s32[]{:S(2)}) async-start(), calls=%async_computation | async-start | bytes 131072 | tf_op jit(solution)/shard_map/psum | solution.py:16
  607.7 1.0 copy-start.2
  609.4 21.4 %collective-permute-start = (bf16[1024,128]{0,1:T(8,128)(2,1)S(1)}, bf16[1024,128]{0,1:T(8,128)(2,1)S(1)}, u32[]{:S(2)}, u32[]{:S(2)}) collective-permute-start(bf16[1024,128]{0,1:T(8,128)(2,1)S(1)} %pad_maximum_fusion.1), channel_id=1, source_target_pairs={{0,509},{1,510},{2,511},{3,0},{4,1},{5,2},{6,3},{7,4},{8,5},{9,6},... | collective-permute-start | bytes 786440 | tf_op jit(solution)/shard_map/ppermute | solution.py:22
  630.9 41.8 %collective-permute-start.1 = (bf16[1024,128]{0,1:T(8,128)(2,1)S(1)}, bf16[1024,128]{0,1:T(8,128)(2,1)S(1)}, u32[]{:S(2)}, u32[]{:S(2)}) collective-permute-start(bf16[1024,128]{0,1:T(8,128)(2,1)S(1)} %collective-permute-done), channel_id=1, source_target_pairs={{0,1},{1,2},{2,3},{3,4},{4,5},{5,6},{6,7},{7,8},{8,9},{9,10},{10,1... | collective-permute-start | bytes 786440 | tf_op jit(solution)/shard_map/ppermute | solution.py:22
  672.7 38.4 %collective-permute-start.2 = (bf16[1024,128]{0,1:T(8,128)(2,1)S(1)}, bf16[1024,128]{0,1:T(8,128)(2,1)S(1)}, u32[]{:S(2)}, u32[]{:S(2)}) collective-permute-start(bf16[1024,128]{0,1:T(8,128)(2,1)S(1)} %collective-permute-done.1), channel_id=1, source_target_pairs={{0,1},{1,2},{2,3},{3,4},{4,5},{5,6},{6,7},{7,8},{8,9},{9,10},{10,1... | collective-permute-start | bytes 786440 | tf_op jit(solution)/shard_map/ppermute | solution.py:22
  711.2 20.8 %collective-permute-start.3 = (bf16[1024,128]{0,1:T(8,128)(2,1)S(1)}, bf16[1024,128]{0,1:T(8,128)(2,1)S(1)}, u32[]{:S(2)}, u32[]{:S(2)}) collective-permute-start(bf16[1024,128]{0,1:T(8,128)(2,1)S(1)} %collective-permute-done.2), channel_id=1, source_target_pairs={{0,2},{1,3},{2,4},{3,5},{4,6},{5,7},{6,8},{7,9},{8,10},{9,11},{10,... | collective-permute-start | bytes 786440 | tf_op jit(solution)/shard_map/ppermute | solution.py:22
  732.1 27.5 %collective-permute-start.4 = (bf16[1024,128]{0,1:T(8,128)(2,1)S(1)}, bf16[1024,128]{0,1:T(8,128)(2,1)S(1)}, u32[]{:S(2)}, u32[]{:S(2)}) collective-permute-start(bf16[1024,128]{0,1:T(8,128)(2,1)S(1)} %collective-permute-done.3), channel_id=1, source_target_pairs={{0,1},{1,2},{2,3},{3,4},{4,5},{5,6},{6,7},{7,8},{8,9},{9,10},{10,1... | collective-permute-start | bytes 786440 | tf_op jit(solution)/shard_map/ppermute | solution.py:22
  759.6 21.1 %collective-permute-start.5 = (bf16[1024,128]{0,1:T(8,128)(2,1)S(1)}, bf16[1024,128]{0,1:T(8,128)(2,1)S(1)}, u32[]{:S(2)}, u32[]{:S(2)}) collective-permute-start(bf16[1024,128]{0,1:T(8,128)(2,1)S(1)} %collective-permute-done.4), channel_id=1, source_target_pairs={{0,1},{1,2},{2,3},{3,4},{4,5},{5,6},{6,7},{7,8},{8,9},{9,10},{10,1... | collective-permute-start | bytes 786440 | tf_op jit(solution)/shard_map/ppermute | solution.py:22
Sparse Core Ops, SparseCore 0:
  144.2 436.9 all-reduce.2
where the time goes:
time: 790 us
  waiting for transfers between devices  567 us (72%)
  blocking collectives  104 us (13%)
  other arithmetic  48.8 us (6%)
  starting transfers between devices  29.5 us (4%)
  matrix products  17.6 us (2%)
  between operations  15.6 us (2%)
    psum x1, waiting for transfers between devices, spread(): return lax.psum(kept, axis)  437 us
    ppermute x6, waiting for transfers between devices, passed_along(): return lax.ppermute(value, axis, pairs)  131 us
    psum x1, blocking collectives, spread(): return lax.psum(kept, axis)  104 us
    ppermute x6, starting transfers between devices, passed_along(): return lax.ppermute(value, axis, pairs)  29.5 us
  transfers between devices with their start and end apart: 7, of which 7 were waited for; matrix products, arithmetic and copies ran while one was open for 1% of the time, Pallas kernels for 0%

commit v1 on v0

--- a/solution.py
+++ b/solution.py
@@ -42,7 +42,7 @@
     second = spread(points[pivots[1]], ("gx", "gy"), owners[1])
     chol_one = jnp.linalg.cholesky(kern(first, first) + jitter * ident)
     first_cols = solve(chol_one, kern(points, first).T, lower=True).T
-    rows = spread(first_cols[pivots[1]], ("gx", "gy"), owners[1])
+    rows = solve(chol_one, kern(second, first).T, lower=True).T
     chol_two = jnp.linalg.cholesky(
         kern(second, second) - jnp.dot(rows, rows.T, precision=hp) + jitter * ident
     )

time: 790 us -> 325 us (0.41)
  the two profiles are of different devices: /device:TPU:225 before, /device:TPU:130 now
where the time goes in v1:
time: 325 us; the launch traced here: 323 us
  waiting for transfers between devices  126 us (39%)
  blocking collectives  104 us (32%)
  other arithmetic  48.3 us (15%)
  starting transfers between devices  20.5 us (6%)
  matrix products  16.2 us (5%)
  local copies, waits for them, and re-layouts  5.55 us (2%)
    ppermute x6, waiting for transfers between devices, passed_along(): return lax.ppermute(value, axis, pairs)  126 us
    psum x1, blocking collectives, spread(): return lax.psum(kept, axis)  104 us
    ppermute x6, starting transfers between devices, passed_along(): return lax.ppermute(value, axis, pairs)  20.5 us
    another operation x3, other arithmetic, shards(): chol_one = jnp.linalg.cholesky(kern(first, first) + jitter * ident)  12.5 us
    another operation x3, other arithmetic, shards(): jnp.linalg.cholesky(kern(second, second) - jnp.dot(rows, rows.T, precisio...  12.4 us
    dot_general x7, matrix products, contribute(): jnp.dot(tile, piece[:, width:], preferred_element_type=jnp.float32)  12 us
    another operation x2, other arithmetic, shards(): second_cols = solve(chol_two, residual_cols.T, lower=True).T  10.6 us
    another operation x2, other arithmetic, shards(): first_cols = solve(chol_one, kern(points, first).T, lower=True).T  10.5 us
  transfers between devices with their start and end apart: 6, of which 6 were waited for; matrix products, arithmetic and copies ran while one was open for 3% of the time, Pallas kernels for 0%

profile of v1, /device:TPU:130, one launch (start us, length us, event | category | flops | bytes accessed | tf_op | source)
XLA Modules:
  0.0 323.0 jit_solution(16918407916820146278)
XLA Ops:
  7.6 104.0 %all-reduce = (bf16[128,64]{1,0:T(8,128)(2,1)S(1)}, bf16[128,64]{1,0:T(8,128)(2,1)S(1)}) all-reduce(bf16[128,64]{1,0:T(8,128)(2,1)S(1)} %broadcast_select_fusion, bf16[128,64]{1,0:T(8,128)(2,1)S(1)} %broadcast_select_fusion.1), channel_id=1, replica_groups=mesh['gx'=32,'gy'=16] {'gx','gy'}, use_global_device_ids=true, to_apply=%region_5.0 | all-reduce | flops 16384 | bytes 65536 | tf_op jit(solution)/shard_map/psum | solution.py:16
  112.9 11.7 %cholesky.44 = f32[128,128]{1,0:T(8,128)S(1)} custom-call(f32[128,128]{1,0:T(8,128)S(1)} %fusion.87), custom_call_target="Cholesky" | custom-call | tf_op jit(solution)/shard_map/jit(cholesky)/cholesky | solution.py:43
  126.3 9.8 %custom-call.11 = f32[1,128,128]{1,2,0:T(8,128)S(1)} custom-call(f32[1,128,128]{2,1,0:T(8,128)S(1)} %copy.14), custom_call_target="InvertDiagBlocksLowerTriangular" | custom-call | tf_op jit(solution)/shard_map/jit(_solve_triangular)/triangular_solve | solution.py:44
  137.4 11.7 %cholesky.55 = f32[128,128]{1,0:T(8,128)S(1)} custom-call(f32[128,128]{1,0:T(8,128)S(1)} %fusion.82), custom_call_target="Cholesky" | custom-call | tf_op jit(solution)/shard_map/jit(cholesky)/cholesky | solution.py:46
  150.5 10.0 %custom-call.12 = f32[1,128,128]{1,2,0:T(8,128)S(1)} custom-call(f32[1,128,128]{2,1,0:T(8,128)S(1)} %fusion.80), custom_call_target="InvertDiagBlocksLowerTriangular" | custom-call | tf_op jit(solution)/shard_map/jit(_solve_triangular)/triangular_solve | solution.py:50
  162.6 5.7 %collective-permute-start = (bf16[1024,128]{0,1:T(8,128)(2,1)S(1)}, bf16[1024,128]{0,1:T(8,128)(2,1)S(1)}, u32[]{:S(2)}, u32[]{:S(2)}) collective-permute-start(bf16[1024,128]{0,1:T(8,128)(2,1)S(1)} %pad_maximum_fusion.1), channel_id=1, source_target_pairs={{0,509},{1,510},{2,511},{3,0},{4,1},{5,2},{6,3},{7,4},{8,5},{9,6},... | collective-permute-start | bytes 786440 | tf_op jit(solution)/shard_map/ppermute | solution.py:22
  169.7 1.4 fusion.24
  171.1 19.0 %collective-permute-done = bf16[1024,128]{0,1:T(8,128)(2,1)S(1)} collective-permute-done((bf16[1024,128]{0,1:T(8,128)(2,1)S(1)}, bf16[1024,128]{0,1:T(8,128)(2,1)S(1)}, u32[]{:S(2)}, u32[]{:S(2)}) %collective-permute-start) | collective-permute-done | bytes 262176 | tf_op jit(solution)/shard_map/ppermute | solution.py:22
  190.2 6.4 %collective-permute-start.1 = (bf16[1024,128]{0,1:T(8,128)(2,1)S(1)}, bf16[1024,128]{0,1:T(8,128)(2,1)S(1)}, u32[]{:S(2)}, u32[]{:S(2)}) collective-permute-start(bf16[1024,128]{0,1:T(8,128)(2,1)S(1)} %collective-permute-done), channel_id=1, source_target_pairs={{0,1},{1,2},{2,3},{3,4},{4,5},{5,6},{6,7},{7,8},{8,9},{9,10},{10,1... | collective-permute-start | bytes 786440 | tf_op jit(solution)/shard_map/ppermute | solution.py:22
  196.6 1.6 fusion.46
  198.2 19.5 %collective-permute-done.1 = bf16[1024,128]{0,1:T(8,128)(2,1)S(1)} collective-permute-done((bf16[1024,128]{0,1:T(8,128)(2,1)S(1)}, bf16[1024,128]{0,1:T(8,128)(2,1)S(1)}, u32[]{:S(2)}, u32[]{:S(2)}) %collective-permute-start.1) | collective-permute-done | bytes 262176 | tf_op jit(solution)/shard_map/ppermute | solution.py:22
  217.7 1.9 collective-permute-start.2
  219.7 1.6 fusion.45
  221.3 23.5 %collective-permute-done.2 = bf16[1024,128]{0,1:T(8,128)(2,1)S(1)} collective-permute-done((bf16[1024,128]{0,1:T(8,128)(2,1)S(1)}, bf16[1024,128]{0,1:T(8,128)(2,1)S(1)}, u32[]{:S(2)}, u32[]{:S(2)}) %collective-permute-start.2) | collective-permute-done | bytes 262176 | tf_op jit(solution)/shard_map/ppermute | solution.py:22
  244.8 1.9 collective-permute-start.3
  246.8 1.6 fusion.44
  248.4 22.6 %collective-permute-done.3 = bf16[1024,128]{0,1:T(8,128)(2,1)S(1)} collective-permute-done((bf16[1024,128]{0,1:T(8,128)(2,1)S(1)}, bf16[1024,128]{0,1:T(8,128)(2,1)S(1)}, u32[]{:S(2)}, u32[]{:S(2)}) %collective-permute-start.3) | collective-permute-done | bytes 262176 | tf_op jit(solution)/shard_map/ppermute | solution.py:22
  271.1 2.4 collective-permute-start.4
  273.5 1.6 fusion.43
  275.2 23.4 %collective-permute-done.4 = bf16[1024,128]{0,1:T(8,128)(2,1)S(1)} collective-permute-done((bf16[1024,128]{0,1:T(8,128)(2,1)S(1)}, bf16[1024,128]{0,1:T(8,128)(2,1)S(1)}, u32[]{:S(2)}, u32[]{:S(2)}) %collective-permute-start.4) | collective-permute-done | bytes 262176 | tf_op jit(solution)/shard_map/ppermute | solution.py:22
  298.6 2.1 collective-permute-start.5
  300.8 1.6 fusion.42
  302.4 18.2 %collective-permute-done.5 = bf16[1024,128]{0,1:T(8,128)(2,1)S(1)} collective-permute-done((bf16[1024,128]{0,1:T(8,128)(2,1)S(1)}, bf16[1024,128]{0,1:T(8,128)(2,1)S(1)}, u32[]{:S(2)}, u32[]{:S(2)}) %collective-permute-start.5) | collective-permute-done | bytes 262176 | tf_op jit(solution)/shard_map/ppermute | solution.py:22
  320.6 2.4 fusion.41
  (49 shorter events, 14.9 us)
Async XLA Ops:
  0.6 161.1 %copy-start = (f32[256,64]{0,1:T(8,128)S(1)}, f32[256,64]{0,1:T(8,128)}, u32[]{:S(2)}) copy-start(f32[256,64]{0,1:T(8,128)} %param.11) | copy-start | bytes 196612
  0.6 111.5 %copy-start.1 = (bf16[1024,64]{0,1:T(8,128)(2,1)S(1)}, bf16[1024,64]{0,1:T(8,128)(2,1)}, u32[]{:S(2)}) copy-start(bf16[1024,64]{0,1:T(8,128)(2,1)} %param.8) | copy-start | bytes 393220
  160.5 1.3 copy-start.2
  162.6 27.5 %collective-permute-start = (bf16[1024,128]{0,1:T(8,128)(2,1)S(1)}, bf16[1024,128]{0,1:T(8,128)(2,1)S(1)}, u32[]{:S(2)}, u32[]{:S(2)}) collective-permute-start(bf16[1024,128]{0,1:T(8,128)(2,1)S(1)} %pad_maximum_fusion.1), channel_id=1, source_target_pairs={{0,509},{1,510},{2,511},{3,0},{4,1},{5,2},{6,3},{7,4},{8,5},{9,6},... | collective-permute-start | bytes 786440 | tf_op jit(solution)/shard_map/ppermute | solution.py:22
  190.2 27.5 %collective-permute-start.1 = (bf16[1024,128]{0,1:T(8,128)(2,1)S(1)}, bf16[1024,128]{0,1:T(8,128)(2,1)S(1)}, u32[]{:S(2)}, u32[]{:S(2)}) collective-permute-start(bf16[1024,128]{0,1:T(8,128)(2,1)S(1)} %collective-permute-done), channel_id=1, source_target_pairs={{0,1},{1,2},{2,3},{3,4},{4,5},{5,6},{6,7},{7,8},{8,9},{9,10},{10,1... | collective-permute-start | bytes 786440 | tf_op jit(solution)/shard_map/ppermute | solution.py:22
  217.7 27.0 %collective-permute-start.2 = (bf16[1024,128]{0,1:T(8,128)(2,1)S(1)}, bf16[1024,128]{0,1:T(8,128)(2,1)S(1)}, u32[]{:S(2)}, u32[]{:S(2)}) collective-permute-start(bf16[1024,128]{0,1:T(8,128)(2,1)S(1)} %collective-permute-done.1), channel_id=1, source_target_pairs={{0,1},{1,2},{2,3},{3,4},{4,5},{5,6},{6,7},{7,8},{8,9},{9,10},{10,1... | collective-permute-start | bytes 786440 | tf_op jit(solution)/shard_map/ppermute | solution.py:22
  244.8 26.2 %collective-permute-start.3 = (bf16[1024,128]{0,1:T(8,128)(2,1)S(1)}, bf16[1024,128]{0,1:T(8,128)(2,1)S(1)}, u32[]{:S(2)}, u32[]{:S(2)}) collective-permute-start(bf16[1024,128]{0,1:T(8,128)(2,1)S(1)} %collective-permute-done.2), channel_id=1, source_target_pairs={{0,2},{1,3},{2,4},{3,5},{4,6},{5,7},{6,8},{7,9},{8,10},{9,11},{10,... | collective-permute-start | bytes 786440 | tf_op jit(solution)/shard_map/ppermute | solution.py:22
  271.1 27.5 %collective-permute-start.4 = (bf16[1024,128]{0,1:T(8,128)(2,1)S(1)}, bf16[1024,128]{0,1:T(8,128)(2,1)S(1)}, u32[]{:S(2)}, u32[]{:S(2)}) collective-permute-start(bf16[1024,128]{0,1:T(8,128)(2,1)S(1)} %collective-permute-done.3), channel_id=1, source_target_pairs={{0,1},{1,2},{2,3},{3,4},{4,5},{5,6},{6,7},{7,8},{8,9},{9,10},{10,1... | collective-permute-start | bytes 786440 | tf_op jit(solution)/shard_map/ppermute | solution.py:22
  298.6 22.0 %collective-permute-start.5 = (bf16[1024,128]{0,1:T(8,128)(2,1)S(1)}, bf16[1024,128]{0,1:T(8,128)(2,1)S(1)}, u32[]{:S(2)}, u32[]{:S(2)}) collective-permute-start(bf16[1024,128]{0,1:T(8,128)(2,1)S(1)} %collective-permute-done.4), channel_id=1, source_target_pairs={{0,1},{1,2},{2,3},{3,4},{4,5},{5,6},{6,7},{7,8},{8,9},{9,10},{10,1... | collective-permute-start | bytes 786440 | tf_op jit(solution)/shard_map/ppermute | solution.py:22

commit v2 on v1

v2 whole, which is shorter than its diff:
```python
import jax
import jax.numpy as jnp
from jax import lax
from jax.experimental import pallas as pl
from jax.experimental.pallas import tpu as pltpu
from jax.sharding import PartitionSpec as P

MESH = pl.DeviceIdType.MESH
F32, BF16 = jnp.float32, jnp.bfloat16
HIGHEST = lax.Precision.HIGHEST

POINTS = 1024
WIDTH = 64
PIVOTS = 128
RANK = 256
SCALE = 32.0
JITTER = 0.1
NOISE_WEIGHT = 0.5
LANES = 128
CHUNK = 128
CHUNKS = POINTS // CHUNK

FIRST_ROUND = (1, 15, 2, 14, 8)
SECOND_ROUND = (5, 11)

SEM_CORE, SEM_Y, SEM_X, SEM_Z, SEM_CORE_BACK = 0, 1, 4, 7, 14
SEM_ZP, SEM_ZN, SEM_OP, SEM_ON, SEM_RP, SEM_RN = 15, 17, 19, 22, 25, 28
SEMS = 31


def dot(a, b, ca=1, cb=0, precision=None):
    return lax.dot_general(
        a, b, (((ca,), (cb,)), ((), ())), precision=precision, preferred_element_type=F32
    )


def three_parts(value):
    high = value.astype(BF16).astype(F32)
    rest = value - high
    middle = rest.astype(BF16).astype(F32)
    return high, middle, rest - middle


def right_columns(points_t):
    count = points_t.shape[1]
    norm = jnp.sum(points_t * points_t, axis=0, keepdims=True) * (-1.0 / SCALE)
    high, middle, low = three_parts(norm)
    row = lax.broadcasted_iota(jnp.int32, (LANES - WIDTH, count), 0)
    extra = jnp.where(row == 0, high, 0.0)
    extra = jnp.where(row == 1, middle, extra)
    extra = jnp.where(row == 2, low, extra)
    extra = jnp.where((row >= 3) & (row < 6), 1.0, extra)
    return extra


def left_columns(points_t):
    count = points_t.shape[1]
    norm = jnp.sum(points_t * points_t, axis=0, keepdims=True) * (-1.0 / SCALE)
    high, middle, low = three_parts(norm)
    row = lax.broadcasted_iota(jnp.int32, (LANES - WIDTH, count), 0)
    extra = jnp.where(row < 3, 1.0, 0.0)
    extra = jnp.where(row == 3, high, extra)
    extra = jnp.where(row == 4, middle, extra)
    extra = jnp.where(row == 5, low, extra)
    return extra


def pivot_rows(value):
    norm = jnp.sum(value * value, axis=1, keepdims=True) * (-1.0 / SCALE)
    high, middle, low = three_parts(norm)
    lane = lax.broadcasted_iota(jnp.int32, value.shape, 1)
    left = value * (2.0 / SCALE)
    left = jnp.where((lane >= 64) & (lane < 67), 1.0, left)
    left = jnp.where(lane == 67, high, left)
    left = jnp.where(lane == 68, middle, left)
    left = jnp.where(lane == 69, low, left)
    right = jnp.where(lane == 64, high, value)
    right = jnp.where(lane == 65, middle, right)
    right = jnp.where(lane == 66, low, right)
    right = jnp.where((lane >= 67) & (lane < 70), 1.0, right)
    return left.astype(BF16), right.astype(BF16)


def inverse_factor(matrix):
    n = PIVOTS
    rows = n // 8
    tiles = [matrix[8 * t : 8 * t + 8, :] for t in range(rows)]
    lane = lax.broadcasted_iota(jnp.int32, (8, n), 1)
    sub = lax.broadcasted_iota(jnp.int32, (8, n), 0)
    for k in range(n):
        top, r = k // 8, k % 8
        pivot_row = jnp.broadcast_to(tiles[top][r : r + 1, :], (8, n))
        pivot = jnp.broadcast_to(tiles[top][r : r + 1, k : k + 1], (8, n))
        scaled = (pivot_row + jnp.where(lane == k, 1.0, 0.0)) * (1.0 / pivot)
        for t in range(top, rows):
            column = jnp.broadcast_to(tiles[t][:, k : k + 1], (8, n))
            if t == top:
                if r == 7:
                    continue
                column = jnp.where(sub > r, column, 0.0)
            tiles[t] = tiles[t] - column * scaled
    out = []
    for t in range(rows):
        diagonal = jnp.sum(jnp.where(lane == sub + 8 * t, tiles[t], 0.0), axis=1, keepdims=True)
        unit = jnp.where(lane < sub + 8 * t, tiles[t], jnp.where(lane == sub + 8 * t, 1.0, 0.0))
        out.append(unit * (1.0 / jnp.sqrt(diagonal)))
    return jnp.concatenate(out, axis=0)


def kernel(
    owners, pivots, points_t, coeffs_t, noise_t, out_t, factor,
    noise_bf, mine, core_buf, stage, y_buf, x_buf, z_buf, pivot_buf, far_points, far_noise,
    near_points, near_noise, left, right, tiles, inverse, probe_bf, probes_t, send, recv,
):
    gx, gy = lax.axis_index("gx"), lax.axis_index("gy")
    core, z_lo, x = gx % 2, (gx // 2) % 4, gx // 8
    z_hi, y = gy // 4, gy % 4
    z = z_hi * 4 + z_lo
    group = gx * 4 + z_hi
    me = gx * 16 + gy

    def at(x, z, core, y):
        return ((x * 4 + z % 4) * 2 + core, (z // 4) * 4 + y)

    def group_at(step):
        other = (group + step + 128) % 128
        return (other // 4, (other % 4) * 4 + y)

    other_core = at(x, z, 1 - core, y)
    y_mates = [at(x, z, core, (y + k) % 4) for k in (1, 2, 3)]
    x_mates = [at((x + k) % 4, z, core, y) for k in (1, 2, 3)]
    z_mates = [at(x, (z + d) % 16, core, y) for d in FIRST_ROUND + SECOND_ROUND]
    after, before = group_at(1), group_at(-1)

    barrier = pltpu.get_barrier_semaphore()
    peers = [other_core] + y_mates + x_mates + z_mates + [after, before]
    for peer in peers:
        pl.semaphore_signal(barrier, inc=1, device_id=peer, device_id_type=MESH)

    def copy(source, target, number, device):
        return pltpu.make_async_remote_copy(
            src_ref=source, dst_ref=target, send_sem=send.at[number], recv_sem=recv.at[number],
            device_id=device, device_id_type=MESH,
        )

    own = points_t[...].astype(F32)
    right[6, 0:WIDTH, :] = points_t[...]
    right[6, WIDTH:, :] = right_columns(own).astype(BF16)
    left[...] = jnp.concatenate([own * (2.0 / SCALE), left_columns(own)], axis=0).T.astype(BF16)
    noise_bf[...] = noise_t[...].astype(BF16)
    index = lax.broadcasted_iota(jnp.int32, (PIVOTS, POINTS), 1)
    for turn in range(2):
        wanted = jnp.where(owners[turn] == me, pivots[turn : turn + 1, :], -1)
        wanted = jnp.broadcast_to(wanted, (PIVOTS, PIVOTS)).T[:, 0:1]
        chosen = jnp.where(index == wanted, 1.0, 0.0).astype(BF16)
        rows = dot(chosen, points_t[...], 1, 1).astype(BF16)
        for half in range(2):
            mine[half, :, WIDTH * turn : WIDTH * (turn + 1)] = rows[64 * half : 64 * half + 64, :]

    pl.semaphore_wait(barrier, len(peers))

    def started(copies):
        for one in copies:
            one.start()
        return copies

    def fill_tile(c, low, high):
        def step(i, carry):
            at_rows = pl.ds(pl.multiple_of(i * CHUNK, CHUNK), CHUNK)
            tiles[c, at_rows, :] = jnp.exp(dot(left[at_rows, :], right[c])).astype(BF16)
            return carry

        lax.fori_loop(low, high, step, 0)

    def fill_right(c):
        block = near_points[c].astype(F32)
        right[c, 0:WIDTH, :] = near_points[c]
        right[c, WIDTH:, :] = right_columns(block).astype(BF16)

    everything = []
    core_copy = started([copy(mine.at[1 - core], core_buf, SEM_CORE, other_core)])
    far_p = started([
        copy(points_t, far_points.at[0], SEM_ZP, after),
        copy(points_t, far_points.at[1], SEM_ZP + 1, before),
    ])
    near_p = started([copy(points_t, near_points.at[k], SEM_OP + k, y_mates[k]) for k in range(3)])
    fill_tile(6, 0, 1)
    core_copy[0].wait_recv()
    stage[0] = mine[core] + core_buf[...]

    x_copies = started([copy(stage.at[0], x_buf.at[k], SEM_X + k, x_mates[k]) for k in range(3)])
    fill_tile(6, 1, 3)
    for one in x_copies:
        one.wait_recv()
    stage[1] = stage[0] + x_buf[0] + x_buf[1] + x_buf[2]

    y_copies = started([copy(stage.at[1], y_buf.at[k], SEM_Y + k, y_mates[k]) for k in range(3)])
    fill_tile(6, 3, 6)
    for one in y_copies:
        one.wait_recv()
    stage[2] = stage[1] + y_buf[0] + y_buf[1] + y_buf[2]

    def either(a, b):
        return jnp.where(a == 0, b, a)

    z_copies = started([
        copy(stage.at[2], z_buf.at[k], SEM_Z + k, z_mates[k]) for k in range(len(FIRST_ROUND))
    ])
    fill_tile(6, 6, 8)
    for k in range(4):
        z_copies[k].wait_recv()
    gathered = stage[2]
    for k in range(4):
        gathered = either(gathered, z_buf[k])
    stage[3] = gathered
    z_more = started([
        copy(stage.at[3], z_buf.at[k], SEM_Z + k, z_mates[k])
        for k in range(len(FIRST_ROUND), len(FIRST_ROUND) + len(SECOND_ROUND))
    ])
    near_n = started([copy(noise_bf, near_noise.at[k], SEM_ON + k, y_mates[k]) for k in range(3)])
    near_p[0].wait_recv()
    fill_right(0)
    fill_tile(0, 0, 4)
    z_copies[4].wait_recv()
    for one in z_more:
        one.wait_recv()
    gathered = stage[3]
    for k in range(4, 7):
        gathered = either(gathered, z_buf[k])
    pivot_buf[core] = gathered
    back = started([copy(pivot_buf.at[core], pivot_buf.at[core], SEM_CORE_BACK, other_core)])
    far_n = started([
        copy(noise_bf, far_noise.at[0], SEM_ZN, after),
        copy(noise_bf, far_noise.at[1], SEM_ZN + 1, before),
    ])
    for one in far_p:
        one.wait_recv()
    which = [1 - (y + k) // 4 for k in (1, 2, 3)]
    relay_p = started([
        copy(far_points.at[which[k]], near_points.at[3 + k], SEM_RP + k, y_mates[k]) for k in range(3)
    ])
    back[0].wait_recv()

    both = jnp.concatenate([pivot_buf[0], pivot_buf[1]], axis=0).astype(F32)
    lane = lax.broadcasted_iota(jnp.int32, both.shape, 1)
    first = jnp.where(lane < WIDTH, both, 0.0)
    second = jnp.where(lane < WIDTH, pltpu.roll(both, WIDTH, 1), 0.0)
    first_left, first_right = pivot_rows(first)
    second_left, second_right = pivot_rows(second)
    square = lax.broadcasted_iota(jnp.int32, (PIVOTS, PIVOTS), 0) == lax.broadcasted_iota(
        jnp.int32, (PIVOTS, PIVOTS), 1
    )
    jitter = jnp.where(square, JITTER, 0.0)
    one_one = jnp.exp(dot(first_left, first_right, 1, 1)) + jitter
    two_one = jnp.exp(dot(second_left, first_right, 1, 1))
    two_two = jnp.exp(dot(second_left, second_right, 1, 1)) + jitter
    inverse_one = inverse_factor(one_one)
    rows = dot(two_one, inverse_one, 1, 1, HIGHEST)
    remainder = two_two - dot(rows, rows, 1, 1, HIGHEST)
    cross = dot(rows, inverse_one, 1, 0, HIGHEST)
    inverse_two = inverse_factor(remainder)
    inverse[0:PIVOTS, 0:PIVOTS] = inverse_one
    inverse[0:PIVOTS, PIVOTS:] = jnp.zeros((PIVOTS, PIVOTS), F32)
    inverse[PIVOTS:, 0:PIVOTS] = -dot(inverse_two, cross, 1, 0, HIGHEST)
    inverse[PIVOTS:, PIVOTS:] = inverse_two

    pivots_left = jnp.concatenate([first_left, second_left], axis=0)
    pivots_right = jnp.concatenate([first_right, second_right], axis=0)
    weights_t = dot(coeffs_t[...], inverse[...], 1, 0, HIGHEST)

    def factor_step(i, carry):
        at_rows = pl.ds(pl.multiple_of(i * CHUNK, CHUNK), CHUNK)
        block = jnp.exp(dot(left[at_rows, :], pivots_right, 1, 1))
        factor[at_rows, :] = dot(block, inverse[...], 1, 1, HIGHEST)
        return carry

    lax.fori_loop(0, CHUNKS, factor_step, 0)

    def probes_of(c):
        columns = jnp.exp(dot(pivots_left, right[c]))
        return dot(weights_t, columns, 1, 0, HIGHEST)

    probes_t[...] = probes_of(6) + noise_t[...]
    probe_bf[6] = probes_t[...].astype(BF16)

    fill_tile(0, 4, 8)
    for k in (1, 2):
        near_p[k].wait_recv()
        fill_right(k)
        fill_tile(k, 0, 8)
    for one in far_n:
        one.wait_recv()
    relay_n = started([
        copy(far_noise.at[which[k]], near_noise.at[3 + k], SEM_RN + k, y_mates[k]) for k in range(3)
    ])
    for k in range(3):
        near_n[k].wait_recv()
        probe_bf[k] = (probes_of(k) + near_noise[k].astype(F32)).astype(BF16)
    for k in range(3):
        relay_p[k].wait_recv()
        fill_right(3 + k)
        fill_tile(3 + k, 0, 8)
    for k in range(3):
        relay_n[k].wait_recv()
        probe_bf[3 + k] = (probes_of(3 + k) + near_noise[3 + k].astype(F32)).astype(BF16)

    def out_step(i, carry):
        at_rows = pl.ds(pl.multiple_of(i * CHUNK, CHUNK), CHUNK)
        total = dot(tiles[0, at_rows, :], probe_bf[0], 1, 1)
        for c in range(1, 7):
            total = total + dot(tiles[c, at_rows, :], probe_bf[c], 1, 1)
        out_t[:, at_rows] = total.T * (1.0 / 32.0) + NOISE_WEIGHT * probes_t[:, at_rows]
        return carry

    lax.fori_loop(0, CHUNKS, out_step, 0)

    for group_of in (core_copy, far_p, near_p, x_copies, y_copies, z_copies, z_more, near_n, back, far_n, relay_p, relay_n):
        for one in group_of:
            one.wait_send()


def shards(points, pivots, owners, coeffs, noise):
    vmem, smem = pl.BlockSpec(memory_space=pltpu.VMEM), pl.BlockSpec(memory_space=pltpu.SMEM)
    block = (WIDTH, POINTS)
    out_t, factor = pl.pallas_call(
        kernel,
        out_shape=(
            jax.ShapeDtypeStruct(block, F32),
            jax.ShapeDtypeStruct((POINTS, RANK), F32),
        ),
        in_specs=[smem, vmem, vmem, vmem, vmem],
        out_specs=(vmem, vmem),
        scratch_shapes=[
            pltpu.VMEM(block, BF16),
            pltpu.VMEM((2, 64, LANES), BF16),
            pltpu.VMEM((64, LANES), BF16),
            pltpu.VMEM((4, 64, LANES), BF16),
            pltpu.VMEM((3, 64, LANES), BF16),
            pltpu.VMEM((3, 64, LANES), BF16),
            pltpu.VMEM((7, 64, LANES), BF16),
            pltpu.VMEM((2, 64, LANES), BF16),
            pltpu.VMEM((2,) + block, BF16),
            pltpu.VMEM((2,) + block, BF16),
            pltpu.VMEM((6,) + block, BF16),
            pltpu.VMEM((6,) + block, BF16),
            pltpu.VMEM((POINTS, LANES), BF16),
            pltpu.VMEM((7, LANES, POINTS), BF16),
            pltpu.VMEM((7, POINTS, POINTS), BF16),
            pltpu.VMEM((RANK, RANK), F32),
            pltpu.VMEM((7,) + block, BF16),
            pltpu.VMEM(block, F32),
            pltpu.SemaphoreType.DMA((SEMS,)),
            pltpu.SemaphoreType.DMA((SEMS,)),
        ],
        compiler_params=pltpu.CompilerParams(
            collective_id=0, has_side_effects=True, vmem_limit_bytes=60 * 1024 * 1024
        ),
    )(owners, pivots, points.T, coeffs.T, noise.T)
    return out_t.T, factor


def solution(mesh):
    in_specs = (P(("gx", "gy"), None), P(), P(), P(), P(("gx", "gy"), None))
    out_specs = (P(("gx", "gy"), None), P(("gx", "gy"), None))
    return jax.shard_map(shards, mesh=mesh, in_specs=in_specs, out_specs=out_specs, check_vma=False)
```

time: 325 us -> 106 us (0.33)
  the two profiles are of different devices: /device:TPU:130 before, /device:TPU:1 now
where the time goes in v2:
time: 106 us
  Pallas kernels  102 us (96%)
  local copies, waits for them, and re-layouts  3.93 us (4%)
    pallas_call x1, Pallas kernels, shards(): pl.pallas_call(kernel, out_shape=(jax.ShapeDtypeStruct(block, F32), jax.S...  102 us
    unnamed x2, local copies, waits for them, and re-layouts  3.93 us

profile of v2, /device:TPU:1, one launch (start us, length us, event | category | flops | bytes accessed | tf_op | source)
XLA Modules:
  0.0 106.2 jit_solution(15196201230546163266)
XLA Ops:
  0.6 101.6 %shard_map.68 = (f32[64,1024]{1,0:T(8,128)}, f32[1024,256]{1,0:T(8,128)}) custom-call(s32[2]{0:T(128)} %owners.1, s32[2,128]{1,0:T(2,128)} %pivots.1, bf16[64,1024]{1,0:T(8,128)(2,1)} %bitcast.6, f32[64,256]{1,0:T(8,128)} %bitcast.7, f32[64,1024]{1,0:T(8,128)} %bitcast.4), custom_call_target="tpu_custom_call" | custom-call | tf_op jit(solution)/shard_map/pallas_call | solution.py:325
  102.3 1.7 %copy.9 = f32[1024,64]{0,1:T(8,128)} copy(f32[1024,64]{0,1:T(8,128)} %bitcast.5) | data formatting | bytes 524288
  103.9 2.3 %copy.10 = f32[1024,256]{1,0:T(8,128)} copy(f32[1024,256]{1,0:T(8,128)} %get-tuple-element.9) | data formatting | bytes 2097152

commit v3 on v2

v3 whole, which is shorter than its diff:
```python
import jax
import jax.numpy as jnp
from jax import lax
from jax.experimental import pallas as pl
from jax.experimental.pallas import tpu as pltpu
from jax.sharding import PartitionSpec as P

MESH = pl.DeviceIdType.MESH
F32, BF16 = jnp.float32, jnp.bfloat16
HIGHEST = lax.Precision.HIGHEST

POINTS = 1024
WIDTH = 64
PIVOTS = 128
RANK = 256
SCALE = 32.0
JITTER = 0.1
NOISE_WEIGHT = 0.5
LANES = 128
CHUNK = 128
CHUNKS = POINTS // CHUNK
TILE_ROWS = 512

FIRST_ROUND = (1, 15, 2, 14, 8)
SECOND_ROUND = (5, 11)

PLUS = ((1, 0), (3, 0), (0, 1), (0, 3))
COVER = ((2, 1), (1, 3), (3, 2))

SEM_CORE, SEM_PLUS, SEM_COVER, SEM_Z, SEM_CORE_BACK = 0, 1, 5, 8, 15
SEM_ZP, SEM_ZN, SEM_OP, SEM_ON, SEM_RP, SEM_RN = 16, 18, 20, 23, 26, 29
SEMS = 32
OUT_ROWS = 256


def dot(a, b, ca=1, cb=0, precision=None):
    return lax.dot_general(
        a, b, (((ca,), (cb,)), ((), ())), precision=precision, preferred_element_type=F32
    )


def three_parts(value):
    high = value.astype(BF16).astype(F32)
    rest = value - high
    middle = rest.astype(BF16).astype(F32)
    return high, middle, rest - middle


def right_columns(points_t):
    count = points_t.shape[1]
    norm = jnp.sum(points_t * points_t, axis=0, keepdims=True) * (-1.0 / SCALE)
    high, middle, low = three_parts(norm)
    row = lax.broadcasted_iota(jnp.int32, (LANES - WIDTH, count), 0)
    extra = jnp.where(row == 0, high, 0.0)
    extra = jnp.where(row == 1, middle, extra)
    extra = jnp.where(row == 2, low, extra)
    extra = jnp.where((row >= 3) & (row < 6), 1.0, extra)
    return extra


def left_columns(points_t):
    count = points_t.shape[1]
    norm = jnp.sum(points_t * points_t, axis=0, keepdims=True) * (-1.0 / SCALE)
    high, middle, low = three_parts(norm)
    row = lax.broadcasted_iota(jnp.int32, (LANES - WIDTH, count), 0)
    extra = jnp.where(row < 3, 1.0, 0.0)
    extra = jnp.where(row == 3, high, extra)
    extra = jnp.where(row == 4, middle, extra)
    extra = jnp.where(row == 5, low, extra)
    return extra


def pivot_rows(value):
    norm = jnp.sum(value * value, axis=1, keepdims=True) * (-1.0 / SCALE)
    high, middle, low = three_parts(norm)
    lane = lax.broadcasted_iota(jnp.int32, value.shape, 1)
    left = value * (2.0 / SCALE)
    left = jnp.where((lane >= 64) & (lane < 67), 1.0, left)
    left = jnp.where(lane == 67, high, left)
    left = jnp.where(lane == 68, middle, left)
    left = jnp.where(lane == 69, low, left)
    right = jnp.where(lane == 64, high, value)
    right = jnp.where(lane == 65, middle, right)
    right = jnp.where(lane == 66, low, right)
    right = jnp.where((lane >= 67) & (lane < 70), 1.0, right)
    return left.astype(BF16), right.astype(BF16)


def reciprocal(value):
    guess = pl.reciprocal(value, approx=True)
    guess = guess * (2.0 - value * guess)
    return guess * (2.0 - value * guess)


def inverse_factor(matrix):
    n = PIVOTS
    count = n // 8
    tiles = [matrix[8 * t : 8 * t + 8, :] for t in range(count)]
    lane = lax.broadcasted_iota(jnp.int32, (8, n), 1)
    sub = lax.broadcasted_iota(jnp.int32, (8, n), 0)
    full = (8, n)
    out = []
    for b in range(count):
        base = 8 * b
        inside = (lane >= base) & (lane < base + 8)
        columns = [jnp.broadcast_to(tiles[b][:, base + j : base + j + 1], full) for j in range(8)]
        s = {
            (i, j): jnp.broadcast_to(columns[j][i : i + 1, :], full)
            for j in range(8)
            for i in range(j, 8)
        }
        panel = jnp.where(inside, jnp.where(lane == sub + base, 1.0, 0.0), tiles[b])
        w = [jnp.broadcast_to(panel[i : i + 1, :], full) for i in range(8)]
        z, m = [None] * 8, {}
        for p in range(0, 8, 2):
            q = p + 1
            a, o, c = s[p, p], s[q, p], s[q, q]
            inv = reciprocal(a * c - o * o)
            for i in range(p + 2, 8):
                m[i, p] = (s[i, p] * c - s[i, q] * o) * inv
                m[i, q] = (s[i, q] * a - s[i, p] * o) * inv
            for i in range(p + 2, 8):
                for j in range(p + 2, i + 1):
                    s[i, j] = s[i, j] - (m[i, p] * s[j, p] + m[i, q] * s[j, q])
            z[p] = (w[p] * c - w[q] * o) * inv
            z[q] = (w[q] * a - w[p] * o) * inv
            for i in range(p + 2, 8):
                w[i] = w[i] - (m[i, p] * w[p] + m[i, q] * w[q])
            ratio = 1.0 / a
            s["first", p] = w[p] * lax.rsqrt(a)
            s["second", p] = (w[q] - o * ratio * w[p]) * lax.rsqrt(c - o * ratio * o)
        for p in (4, 2, 0):
            for j in (p, p + 1):
                for i in range(p + 2, 8):
                    z[j] = z[j] - m[i, j] * z[i]
        for t in range(b + 1, count):
            now = jnp.where(inside, 0.0, tiles[t])
            parts = [
                jnp.broadcast_to(tiles[t][:, base + j : base + j + 1], full) * z[j] for j in range(8)
            ]
            while len(parts) > 1:
                parts = [parts[i] + parts[i + 1] for i in range(0, len(parts), 2)]
            tiles[t] = now - parts[0]
        done = s["first", 0]
        for i in range(1, 8):
            done = jnp.where(sub == i, s["first" if i % 2 == 0 else "second", i - i % 2], done)
        out.append(jnp.where(lane < base + 8, done, 0.0))
    return jnp.concatenate(out, axis=0)


def kernel(
    owners, pivots, points_hbm, coeffs_hbm, noise_hbm, out_hbm, left_hbm, right_hbm, inverse_hbm,
    out_t, left, pivots_right, inverse, points_t, coeffs_t, noise_t, noise_bf, mine, core_buf, stage, plus_buf, cover_buf, z_buf, pivot_buf, far_points, far_noise,
    near_points, near_noise, right, tiles, probe_bf, probes_t, totals, send, recv, loaded, saved,
):
    loads = [
        pltpu.make_async_copy(source, target, loaded.at[i])
        for i, (source, target) in enumerate(
            ((points_hbm, points_t), (noise_hbm, noise_t), (coeffs_hbm, coeffs_t))
        )
    ]
    for load in loads:
        load.start()
    gx, gy = lax.axis_index("gx"), lax.axis_index("gy")
    core, z_lo, x = gx % 2, (gx // 2) % 4, gx // 8
    z_hi, y = gy // 4, gy % 4
    z = z_hi * 4 + z_lo
    group = gx * 4 + z_hi
    me = gx * 16 + gy

    def at(x, z, core, y):
        return (((x % 4) * 4 + z % 4) * 2 + core, (z // 4) * 4 + y % 4)

    def group_at(step):
        other = (group + step + 128) % 128
        return (other // 4, (other % 4) * 4 + y)

    other_core = at(x, z, 1 - core, y)
    y_mates = [at(x, z, core, y + k) for k in (1, 2, 3)]
    plus_mates = [at(x + i, z, core, y + j) for i, j in PLUS]
    cover_mates = [at(x + i, z, core, y + j) for i, j in COVER]
    cover_sources = [at(x + 4 - i, z, core, y + 4 - j) for i, j in COVER]
    z_mates = [at(x, (z + d) % 16, core, y) for d in FIRST_ROUND + SECOND_ROUND]
    after, before = group_at(1), group_at(-1)

    barrier = pltpu.get_barrier_semaphore()
    peers = [other_core] + plus_mates[0:2] + y_mates + cover_sources + z_mates + [after, before]
    for peer in peers:
        pl.semaphore_signal(barrier, inc=1, device_id=peer, device_id_type=MESH)

    def copy(source, target, number, device):
        return pltpu.make_async_remote_copy(
            src_ref=source, dst_ref=target, send_sem=send.at[number], recv_sem=recv.at[number],
            device_id=device, device_id_type=MESH,
        )

    def started(copies):
        for one in copies:
            one.start()
        return copies

    def arrived(copies):
        for one in copies:
            one.wait_recv()

    def either(a, b):
        return jnp.where(a == 0, b, a)

    def fill_tile(c, low=0, high=POINTS // TILE_ROWS):
        def step(i, carry):
            at_rows = pl.ds(pl.multiple_of(i * TILE_ROWS, TILE_ROWS), TILE_ROWS)
            tiles[c, at_rows, :] = jnp.exp(dot(left[at_rows, :], right[c])).astype(BF16)
            return carry

        lax.fori_loop(low, high, step, 0)

    def fill_right(c):
        block = near_points[c].astype(F32)
        right[c, 0:WIDTH, :] = near_points[c]
        right[c, WIDTH:, :] = right_columns(block).astype(BF16)

    loads[0].wait()
    index = lax.broadcasted_iota(jnp.int32, (PIVOTS, POINTS), 1)
    for turn in range(2):
        wanted = jnp.where(owners[turn] == me, pivots[turn : turn + 1, :], -1)
        wanted = jnp.broadcast_to(wanted, (PIVOTS, PIVOTS)).T[:, 0:1]
        chosen = jnp.where(index == wanted, 1.0, 0.0).astype(BF16)
        rows = dot(chosen, points_t[...], 1, 1).astype(BF16)
        for half in range(2):
            mine[half, :, WIDTH * turn : WIDTH * (turn + 1)] = rows[64 * half : 64 * half + 64, :]

    pl.semaphore_wait(barrier, len(peers))

    def save(source, target, number):
        one = pltpu.make_async_copy(source, target, saved.at[number])
        one.start()
        return one

    core_copy = started([copy(mine.at[1 - core], core_buf, SEM_CORE, other_core)])
    near_p = started([copy(points_t, near_points.at[k], SEM_OP + k, y_mates[k]) for k in range(3)])

    own = points_t[...].astype(F32)
    right[6, 0:WIDTH, :] = points_t[...]
    right[6, WIDTH:, :] = right_columns(own).astype(BF16)
    left[...] = jnp.concatenate([own * (2.0 / SCALE), left_columns(own)], axis=0).T.astype(BF16)
    saves = [save(left, left_hbm, 0)]
    loads[1].wait()
    noise_bf[...] = noise_t[...].astype(BF16)
    loads[2].wait()

    arrived(core_copy)
    stage[0] = mine[core] + core_buf[...]

    rounds = len(FIRST_ROUND)
    z_first = started([copy(stage.at[0], z_buf.at[k], SEM_Z + k, z_mates[k]) for k in range(rounds)])
    fill_tile(6, 0, 1)
    arrived(z_first[0:4])
    gathered = stage[0]
    for k in range(4):
        gathered = either(gathered, z_buf[k])
    stage[1] = gathered
    z_second = started([
        copy(stage.at[1], z_buf.at[rounds + k], SEM_Z + rounds + k, z_mates[rounds + k])
        for k in range(len(SECOND_ROUND))
    ])
    fill_tile(6, 1, 2)
    arrived(z_first[4:])
    arrived(z_second)
    gathered = stage[1]
    for k in range(4, 7):
        gathered = either(gathered, z_buf[k])
    stage[2] = gathered
    plus = started([copy(stage.at[2], plus_buf.at[k], SEM_PLUS + k, plus_mates[k]) for k in range(4)])
    far_p = started([
        copy(points_t, far_points.at[0], SEM_ZP, after),
        copy(points_t, far_points.at[1], SEM_ZP + 1, before),
    ])
    arrived(near_p[2:])
    fill_right(2)
    fill_tile(2, 0, 1)
    arrived(plus)
    gathered = stage[2]
    for k in range(4):
        gathered = either(gathered, plus_buf[k])
    stage[3] = gathered
    cover = started([copy(stage.at[3], cover_buf.at[k], SEM_COVER + k, cover_mates[k]) for k in range(3)])
    fill_tile(2, 1, 2)
    arrived(near_p[0:1])
    fill_right(0)
    fill_tile(0)
    arrived(cover)
    gathered = stage[3]
    for k in range(3):
        gathered = either(gathered, cover_buf[k])
    pivot_buf[core] = gathered
    back = started([copy(pivot_buf.at[core], pivot_buf.at[core], SEM_CORE_BACK, other_core)])
    near_n = started([copy(noise_bf, near_noise.at[k], SEM_ON + k, y_mates[k]) for k in range(3)])
    far_n = started([
        copy(noise_bf, far_noise.at[0], SEM_ZN, after),
        copy(noise_bf, far_noise.at[1], SEM_ZN + 1, before),
    ])
    arrived(near_p[1:2])
    fill_right(1)
    fill_tile(1)
    arrived(back)

    both = jnp.concatenate([pivot_buf[0], pivot_buf[1]], axis=0).astype(F32)
    lane = lax.broadcasted_iota(jnp.int32, both.shape, 1)
    first = jnp.where(lane < WIDTH, both, 0.0)
    second = jnp.where(lane < WIDTH, pltpu.roll(both, WIDTH, 1), 0.0)
    first_left, first_right = pivot_rows(first)
    second_left, second_right = pivot_rows(second)
    square = lax.broadcasted_iota(jnp.int32, (PIVOTS, PIVOTS), 0) == lax.broadcasted_iota(
        jnp.int32, (PIVOTS, PIVOTS), 1
    )
    jitter = jnp.where(square, JITTER, 0.0)
    one_one = jnp.exp(dot(first_left, first_right, 1, 1)) + jitter
    two_one = jnp.exp(dot(second_left, first_right, 1, 1))
    two_two = jnp.exp(dot(second_left, second_right, 1, 1)) + jitter
    inverse_one = inverse_factor(one_one)
    inverse[0:PIVOTS, 0:PIVOTS] = inverse_one

    arrived(far_p)
    which = [1 - (y + k) // 4 for k in (1, 2, 3)]
    relay_p = started([
        copy(far_points.at[which[k]], near_points.at[3 + k], SEM_RP + k, y_mates[k]) for k in range(3)
    ])

    rows = dot(two_one, inverse_one, 1, 1, HIGHEST)
    remainder = two_two - dot(rows, rows, 1, 1, HIGHEST)
    cross = dot(rows, inverse_one, 1, 0, HIGHEST)
    inverse_two = inverse_factor(remainder)
    inverse[0:PIVOTS, PIVOTS:] = jnp.zeros((PIVOTS, PIVOTS), F32)
    inverse[PIVOTS:, 0:PIVOTS] = -dot(inverse_two, cross, 1, 0, HIGHEST)
    inverse[PIVOTS:, PIVOTS:] = inverse_two
    saves.append(save(inverse, inverse_hbm, 1))
    pivots_right[...] = jnp.concatenate([first_right, second_right], axis=0)
    saves.append(save(pivots_right, right_hbm, 2))
    pivots_left = jnp.concatenate([first_left, second_left], axis=0)
    weights_t = dot(coeffs_t[...], inverse[...], 1, 0, HIGHEST)
    weights = jnp.concatenate(three_parts(weights_t), axis=0).astype(BF16)

    def probes_of(c):
        high, middle, low = three_parts(jnp.exp(dot(pivots_left, right[c])))
        one = dot(weights, high.astype(BF16))
        two = dot(weights[0 : 2 * WIDTH], middle.astype(BF16))
        three = dot(weights[0:WIDTH], low.astype(BF16))
        small = one[2 * WIDTH :] + two[WIDTH:] + three
        return one[0:WIDTH] + ((one[WIDTH : 2 * WIDTH] + two[0:WIDTH]) + small)

    probes_t[...] = probes_of(6) + noise_t[...]
    probe_bf[6] = probes_t[...].astype(BF16)
    for k in range(3):
        arrived(near_n[k : k + 1])
        probe_bf[k] = (probes_of(k) + near_noise[k].astype(F32)).astype(BF16)

    arrived(far_n)
    relay_n = started([
        copy(far_noise.at[which[k]], near_noise.at[3 + k], SEM_RN + k, y_mates[k]) for k in range(3)
    ])

    def near_step(i, carry):
        at_rows = pl.ds(pl.multiple_of(i * OUT_ROWS, OUT_ROWS), OUT_ROWS)
        total = dot(tiles[6, at_rows, :], probe_bf[6], 1, 1)
        for c in range(3):
            total = total + dot(tiles[c, at_rows, :], probe_bf[c], 1, 1)
        totals[at_rows, :] = total
        return carry

    lax.fori_loop(0, POINTS // OUT_ROWS, near_step, 0)

    for k in (2, 0, 1):
        arrived(relay_p[k : k + 1])
        fill_right(3 + k)
        fill_tile(3 + k)
    for k in (2, 0, 1):
        arrived(relay_n[k : k + 1])
        probe_bf[3 + k] = (probes_of(3 + k) + near_noise[3 + k].astype(F32)).astype(BF16)

    def far_step(i, carry):
        at_rows = pl.ds(pl.multiple_of(i * OUT_ROWS, OUT_ROWS), OUT_ROWS)
        total = totals[at_rows, :]
        for c in range(3, 6):
            total = total + dot(tiles[c, at_rows, :], probe_bf[c], 1, 1)
        out_t[:, at_rows] = total.T * (1.0 / 32.0) + NOISE_WEIGHT * probes_t[:, at_rows]
        return carry

    lax.fori_loop(0, POINTS // OUT_ROWS, far_step, 0)
    saves.append(save(out_t, out_hbm, 3))

    for copies in (
        core_copy, near_p, z_first, z_second, plus, far_p, cover, back, near_n, far_n, relay_p, relay_n
    ):
        for one in copies:
            one.wait_send()
    for one in saves:
        one.wait()


def factor_kernel(left, pivots_right, inverse, given_t, factor, out_t):
    block = jnp.exp(dot(left[...], pivots_right[...], 1, 1))
    factor[...] = dot(block, inverse[...], 1, 1, HIGHEST)
    out_t[...] = given_t[...]


def shards(points, pivots, owners, coeffs, noise):
    vmem, smem = pl.BlockSpec(memory_space=pltpu.VMEM), pl.BlockSpec(memory_space=pltpu.SMEM)
    anywhere = pl.BlockSpec(memory_space=pl.ANY)
    block = (WIDTH, POINTS)
    part = (64, LANES)
    given_t, left, pivots_right, inverse = pl.pallas_call(
        kernel,
        out_shape=(
            jax.ShapeDtypeStruct(block, F32),
            jax.ShapeDtypeStruct((POINTS, LANES), BF16),
            jax.ShapeDtypeStruct((RANK, LANES), BF16),
            jax.ShapeDtypeStruct((RANK, RANK), F32),
        ),
        in_specs=[smem, vmem, anywhere, anywhere, anywhere],
        out_specs=(anywhere, anywhere, anywhere, anywhere),
        scratch_shapes=[
            pltpu.VMEM(block, F32),
            pltpu.VMEM((POINTS, LANES), BF16),
            pltpu.VMEM((RANK, LANES), BF16),
            pltpu.VMEM((RANK, RANK), F32),
            pltpu.VMEM(block, BF16),
            pltpu.VMEM((WIDTH, RANK), F32),
            pltpu.VMEM(block, F32),
            pltpu.VMEM(block, BF16),
            pltpu.VMEM((2,) + part, BF16),
            pltpu.VMEM(part, BF16),
            pltpu.VMEM((4,) + part, BF16),
            pltpu.VMEM((4,) + part, BF16),
            pltpu.VMEM((3,) + part, BF16),
            pltpu.VMEM((7,) + part, BF16),
            pltpu.VMEM((2,) + part, BF16),
            pltpu.VMEM((2,) + block, BF16),
            pltpu.VMEM((2,) + block, BF16),
            pltpu.VMEM((6,) + block, BF16),
            pltpu.VMEM((6,) + block, BF16),
            pltpu.VMEM((7, LANES, POINTS), BF16),
            pltpu.VMEM((7, POINTS, POINTS), BF16),
            pltpu.VMEM((7,) + block, BF16),
            pltpu.VMEM(block, F32),
            pltpu.VMEM((POINTS, WIDTH), F32),
            pltpu.SemaphoreType.DMA((SEMS,)),
            pltpu.SemaphoreType.DMA((SEMS,)),
            pltpu.SemaphoreType.DMA((3,)),
            pltpu.SemaphoreType.DMA((4,)),
        ],
        compiler_params=pltpu.CompilerParams(
            collective_id=0, has_side_effects=True, vmem_limit_bytes=62 * 1024 * 1024
        ),
    )(owners, pivots, points.T, coeffs.T, noise.T)
    steps = 4
    tall = POINTS // steps
    factor, out_t = pl.pallas_call(
        factor_kernel,
        grid=(steps,),
        out_shape=(
            jax.ShapeDtypeStruct((POINTS, RANK), F32),
            jax.ShapeDtypeStruct(block, F32),
        ),
        in_specs=[
            pl.BlockSpec((tall, LANES), lambda i: (i, 0)),
            pl.BlockSpec((RANK, LANES), lambda i: (0, 0)),
            pl.BlockSpec((RANK, RANK), lambda i: (0, 0)),
            pl.BlockSpec((WIDTH, tall), lambda i: (0, i)),
        ],
        out_specs=(
            pl.BlockSpec((tall, RANK), lambda i: (i, 0)),
            pl.BlockSpec((WIDTH, tall), lambda i: (0, i)),
        ),
        compiler_params=pltpu.CompilerParams(vmem_limit_bytes=62 * 1024 * 1024),
    )(left, pivots_right, inverse, given_t)
    return out_t.T, factor


def solution(mesh):
    in_specs = (P(("gx", "gy"), None), P(), P(), P(), P(("gx", "gy"), None))
    out_specs = (P(("gx", "gy"), None), P(("gx", "gy"), None))
    return jax.shard_map(shards, mesh=mesh, in_specs=in_specs, out_specs=out_specs, check_vma=False)
```

time: 106 us -> 72.2 us (0.68)
  Pallas kernels: 102 us -> 71.3 us
  local copies, waits for them, and re-layouts: 3.93 us -> 0 us
    pallas_call x1, Pallas kernels: 102 us -> 66.9 us  [shards(): pl.pallas_call(kernel, out_shape=(jax.ShapeDtypeStruct(block, F32), jax.S...]
    pallas_call x0 -> x1, Pallas kernels: none -> 4.42 us  [shards(): pl.pallas_call(factor_kernel, grid=(steps,), out_shape=(jax.ShapeDtypeStr...]
    unnamed x2 -> x0, local copies, waits for them, and re-layouts: 3.93 us -> none
where the time goes in v3:
time: 72.2 us; the launch traced here: 72 us
  Pallas kernels  71.3 us (99%)
    pallas_call x1, Pallas kernels, shards(): pl.pallas_call(kernel, out_shape=(jax.ShapeDtypeStruct(block, F32), jax.S...  66.9 us
    pallas_call x1, Pallas kernels, shards(): pl.pallas_call(factor_kernel, grid=(steps,), out_shape=(jax.ShapeDtypeStr...  4.42 us

profile of v3, /device:TPU:1, one launch (start us, length us, event | category | flops | bytes accessed | tf_op | source)
XLA Modules:
  0.0 72.0 jit_solution(18021704910409793813)
XLA Ops:
  0.6 66.9 %shard_map.68 = (f32[64,1024]{1,0:T(8,128)}, bf16[1024,128]{1,0:T(8,128)(2,1)}, bf16[256,128]{1,0:T(8,128)(2,1)}, f32[256,256]{1,0:T(8,128)}) custom-call(s32[2]{0:T(128)} %owners.1, s32[2,128]{1,0:T(2,128)} %pivots.1, bf16[64,1024]{1,0:T(8,128)(2,1)} %bitcast.5, f32[64,256]{1,0:T(8,128)} %bitcast.6, f32[64,1024]{1,0:T(8,128)} %bitcast.4), custom_call_target="tpu_custom_call" | custom-call | tf_op jit(solution)/shard_map/pallas_call | solution.py:411
  67.5 4.4 %shard_map.69 = (f32[1024,256]{1,0:T(8,128)}, f32[64,1024]{1,0:T(8,128)}) custom-call(bf16[1024,128]{1,0:T(8,128)(2,1)} %get-tuple-element.8.left, bf16[256,128]{1,0:T(8,128)(2,1)} %get-tuple-element.9.pivots_right, f32[256,256]{1,0:T(8,128)} %get-tuple-element.10.inverse, f32[64,1024]{1,0:T(8,128)} %get-tuple-element.11.given_t), custom_call_target="tpu_custom_call" | custom-call | tf_op jit(solution)/shard_map/pallas_call | solution.py:457

commit v4 on v3

--- a/solution.py
+++ b/solution.py
@@ -29,7 +29,8 @@
 
 SEM_CORE, SEM_PLUS, SEM_COVER, SEM_Z, SEM_CORE_BACK = 0, 1, 5, 8, 15
 SEM_ZP, SEM_ZN, SEM_OP, SEM_ON, SEM_RP, SEM_RN = 16, 18, 20, 23, 26, 29
-SEMS = 32
+SEM_PASS = 32
+SEMS = 33
 OUT_ROWS = 256
 
 
@@ -151,7 +152,7 @@
 def kernel(
     owners, pivots, points_hbm, coeffs_hbm, noise_hbm, out_hbm, left_hbm, right_hbm, inverse_hbm,
     out_t, left, pivots_right, inverse, points_t, coeffs_t, noise_t, noise_bf, mine, core_buf, stage, plus_buf, cover_buf, z_buf, pivot_buf, far_points, far_noise,
-    near_points, near_noise, right, tiles, probe_bf, probes_t, totals, send, recv, loaded, saved,
+    near_points, near_noise, right, tiles, probe_bf, probes_t, totals, far_probes, send, recv, loaded, saved,
 ):
     loads = [
         pltpu.make_async_copy(source, target, loaded.at[i])
@@ -263,6 +264,10 @@
         copy(stage.at[1], z_buf.at[rounds + k], SEM_Z + rounds + k, z_mates[rounds + k])
         for k in range(len(SECOND_ROUND))
     ])
+    far_p = started([
+        copy(points_t, far_points.at[0], SEM_ZP, after),
+        copy(points_t, far_points.at[1], SEM_ZP + 1, before),
+    ])
     fill_tile(6, 1, 2)
     arrived(z_first[4:])
     arrived(z_second)
@@ -271,10 +276,6 @@
         gathered = either(gathered, z_buf[k])
     stage[2] = gathered
     plus = started([copy(stage.at[2], plus_buf.at[k], SEM_PLUS + k, plus_mates[k]) for k in range(4)])
-    far_p = started([
-        copy(points_t, far_points.at[0], SEM_ZP, after),
-        copy(points_t, far_points.at[1], SEM_ZP + 1, before),
-    ])
     arrived(near_p[2:])
     fill_right(2)
     fill_tile(2, 0, 1)
@@ -294,7 +295,7 @@
         gathered = either(gathered, cover_buf[k])
     pivot_buf[core] = gathered
     back = started([copy(pivot_buf.at[core], pivot_buf.at[core], SEM_CORE_BACK, other_core)])
-    near_n = started([copy(noise_bf, near_noise.at[k], SEM_ON + k, y_mates[k]) for k in range(3)])
+    near_n = started([copy(noise_bf, near_noise.at[k], SEM_ON + k, y_mates[k]) for k in (0, 2)])
     far_n = started([
         copy(noise_bf, far_noise.at[0], SEM_ZN, after),
         copy(noise_bf, far_noise.at[1], SEM_ZN + 1, before),
@@ -320,6 +321,12 @@
     inverse_one = inverse_factor(one_one)
     inverse[0:PIVOTS, 0:PIVOTS] = inverse_one
 
+    arrived(near_n)
+    upper, lower = pl.ds(0, WIDTH // 2), pl.ds(WIDTH // 2, WIDTH // 2)
+    passed = started([
+        copy(near_noise.at[0, upper], near_noise.at[1, upper], SEM_ON + 1, y_mates[0]),
+        copy(near_noise.at[2, lower], near_noise.at[1, lower], SEM_PASS, y_mates[2]),
+    ])
     arrived(far_p)
     which = [1 - (y + k) // 4 for k in (1, 2, 3)]
     relay_p = started([
@@ -350,8 +357,9 @@
 
     probes_t[...] = probes_of(6) + noise_t[...]
     probe_bf[6] = probes_t[...].astype(BF16)
-    for k in range(3):
-        arrived(near_n[k : k + 1])
+    for k in (0, 2, 1):
+        if k == 1:
+            arrived(passed)
         probe_bf[k] = (probes_of(k) + near_noise[k].astype(F32)).astype(BF16)
 
     arrived(far_n)
@@ -373,9 +381,10 @@
         arrived(relay_p[k : k + 1])
         fill_right(3 + k)
         fill_tile(3 + k)
+        far_probes[k] = probes_of(3 + k)
     for k in (2, 0, 1):
         arrived(relay_n[k : k + 1])
-        probe_bf[3 + k] = (probes_of(3 + k) + near_noise[3 + k].astype(F32)).astype(BF16)
+        probe_bf[3 + k] = (far_probes[k] + near_noise[3 + k].astype(F32)).astype(BF16)
 
     def far_step(i, carry):
         at_rows = pl.ds(pl.multiple_of(i * OUT_ROWS, OUT_ROWS), OUT_ROWS)
@@ -389,7 +398,7 @@
     saves.append(save(out_t, out_hbm, 3))
 
     for copies in (
-        core_copy, near_p, z_first, z_second, plus, far_p, cover, back, near_n, far_n, relay_p, relay_n
+        core_copy, near_p, z_first, z_second, plus, far_p, cover, back, near_n, far_n, relay_p, relay_n, passed
     ):
         for one in copies:
             one.wait_send()
@@ -443,6 +452,7 @@
             pltpu.VMEM((7,) + block, BF16),
             pltpu.VMEM(block, F32),
             pltpu.VMEM((POINTS, WIDTH), F32),
+            pltpu.VMEM((3,) + block, F32),
             pltpu.SemaphoreType.DMA((SEMS,)),
             pltpu.SemaphoreType.DMA((SEMS,)),
             pltpu.SemaphoreType.DMA((3,)),

time: 72.2 us -> 69.9 us (0.968)
  Pallas kernels: 71.3 us -> 68.9 us
    pallas_call x1, Pallas kernels: 66.9 us -> 64.5 us  [shards(): pl.pallas_call(kernel, out_shape=(jax.ShapeDtypeStruct(block, F32), jax.S...]
where the time goes in v4:
time: 69.9 us; the launch traced here: 69.6 us
  Pallas kernels  68.9 us (99%)
    pallas_call x1, Pallas kernels, shards(): pl.pallas_call(kernel, out_shape=(jax.ShapeDtypeStruct(block, F32), jax.S...  64.5 us
    pallas_call x1, Pallas kernels, shards(): pl.pallas_call(factor_kernel, grid=(steps,), out_shape=(jax.ShapeDtypeStr...  4.43 us

profile of v4, /device:TPU:1, one launch (start us, length us, event | category | flops | bytes accessed | tf_op | source)
XLA Modules:
  0.0 69.6 jit_solution(17339839118484587667)
XLA Ops:
  0.6 64.5 %shard_map.68 = (f32[64,1024]{1,0:T(8,128)}, bf16[1024,128]{1,0:T(8,128)(2,1)}, bf16[256,128]{1,0:T(8,128)(2,1)}, f32[256,256]{1,0:T(8,128)}) custom-call(s32[2]{0:T(128)} %owners.1, s32[2,128]{1,0:T(2,128)} %pivots.1, bf16[64,1024]{1,0:T(8,128)(2,1)} %bitcast.5, f32[64,256]{1,0:T(8,128)} %bitcast.6, f32[64,1024]{1,0:T(8,128)} %bitcast.4), custom_call_target="tpu_custom_call" | custom-call | tf_op jit(solution)/shard_map/pallas_call | solution.py:420
  65.1 4.4 %shard_map.69 = (f32[1024,256]{1,0:T(8,128)}, f32[64,1024]{1,0:T(8,128)}) custom-call(bf16[1024,128]{1,0:T(8,128)(2,1)} %get-tuple-element.8.left, bf16[256,128]{1,0:T(8,128)(2,1)} %get-tuple-element.9.pivots_right, f32[256,256]{1,0:T(8,128)} %get-tuple-element.10.inverse, f32[64,1024]{1,0:T(8,128)} %get-tuple-element.11.given_t), custom_call_target="tpu_custom_call" | custom-call | tf_op jit(solution)/shard_map/pallas_call | solution.py:467
